TPU v7x, 256 devices: a whole 4x4x8 slice. The times are simulated.
256 devices in a mesh: gx: 32 (over y, z), gy: 8 (over x, core).
Axes of the slice: x: 4, y: 4, z: 8, core: 2. Of those that a mesh axis runs over, the one named last changes fastest.
Arguments:
- densities: bfloat16 [24576, 32, 128], P(('gx', 'gy')), may hold values from -6 to 6
- geometry: float32 [24576, 7, 128], P(('gx', 'gy')), as said below
- near_ids: int32 [24576, 8], P(('gx', 'gy')), may hold values from 0 to 24575, as said below
- basis_in: bfloat16 [24576, 64, 128], P(('gx', 'gy')), may hold values from -0.5 to 0.5
- basis_out: bfloat16 [24576, 64, 128], P(('gx', 'gy')), may hold values from -0.75 to 0.75
- leaf_up: bfloat16 [24576, 64, 64], P(('gx', 'gy')), may hold values from -0.078125 to 0.078125
- leaf_down: bfloat16 [24576, 64, 64], P(('gx', 'gy')), may hold values from -0.75 to 0.75
- leaf_coupling: bfloat16 [24576, 6, 64, 64], P(('gx', 'gy')), may hold values from -0.3125 to 0.3125
- leaf_far: int32 [24576, 6], P(('gx', 'gy')), may hold values from 0 to 24575, as said below
- leaf_count: int32 [24576], P(('gx', 'gy')), may hold values from 1 to 6, as said below
- cluster_up: bfloat16 [256, 64, 64], P(('gx', 'gy')), may hold values from -0.25 to 0.25
- cluster_down: bfloat16 [256, 64, 64], P(('gx', 'gy')), may hold values from -0.75 to 0.75
- cluster_coupling: bfloat16 [256, 6, 64, 64], P(('gx', 'gy')), may hold values from -0.3125 to 0.3125
- cluster_far: int32 [256, 6], P(('gx', 'gy')), may hold values from 0 to 255, as said below
- group_up: bfloat16 [32, 64, 64], replicated, may hold values from -0.375 to 0.375
- group_down: bfloat16 [32, 64, 64], P('gx'), may hold values from -0.75 to 0.75
- group_coupling: bfloat16 [32, 6, 64, 64], P('gx'), may hold values from -0.3125 to 0.3125
- group_far: int32 [32, 6], P('gx'), may hold values from 0 to 31, as said below
- root_coupling: bfloat16 [8, 8, 64, 64], replicated, may hold values from -0.25 to 0.25
Outputs:
- potential: float32 [24576, 32, 128], P(('gx', 'gy'))
Inputs may be any that keep to these rules, and one draw needn't show every extreme that they name: `near_ids`: row l names 8 different leaves of a window of 9 consecutive leaves that contains l, centred on l where the ends allow. `leaf_far`: row l names 6 different leaves held by l's device or its two neighbours in leaf order, none within 4 leaves of l; only the first leaf_count[l] entries are used. `leaf_count`: every device holds a leaf with 6. `cluster_far`: row u names 6 different level-two clusters other than u, of u's group or the two groups beside it. `group_far`: row g names 6 different level-one clusters other than g. `geometry`: rows 0 to 2 hold a panel's centre, rows 3 to 5 its unit normal, row 6 its area, from 0.25 to 2.
All inputs are finite; a program needn't handle non-finite values.
Results may differ from a plain program's by a relative error of at most 0.012.
Values may be sent and summed in bfloat16 or wider, within the bound.
A program may use at most 128 MiB of HBM per device.

v0:
```python
import math
import jax
import jax.numpy as jnp
from jax import lax
from jax.sharding import PartitionSpec as P

REACH = 4
BRANCH = 4
four_pi = 4.0 * math.pi
leaf_block = 8


def padded(cells, sides, width):
    for axis, dim in sides:
        count = lax.axis_size(axis)
        ends = count - 1
        head = lax.slice_in_dim(cells, 0, width, axis=dim)
        tail = lax.slice_in_dim(cells, cells.shape[dim] - width, cells.shape[dim], axis=dim)
        cells = jnp.concatenate(
            [
                lax.ppermute(tail, axis, [(i, (i + 1) % count) for i in range(ends)]),
                cells,
                lax.ppermute(head, axis, [((i + 1) % count, i) for i in range(ends)]),
            ],
            axis=dim,
        )
    return cells


def near_kernel(target, source):
    offsets = [
        target[:, coord_id, :, None, None] - source[:, None, :, coord_id, :]
        for coord_id in range(3)
    ]
    distance = offsets[0] * offsets[0] + offsets[1] * offsets[1] + offsets[2] * offsets[2]
    facing = (
        source[:, None, :, 3, :] * offsets[0]
        + source[:, None, :, 4, :] * offsets[1]
        + source[:, None, :, 5, :] * offsets[2]
    )
    panel_area = source[:, None, :, 6, :]
    spread = distance + panel_area
    return panel_area * facing / (four_pi * spread * jnp.sqrt(spread))


def on_device(
    densities,
    geometry,
    near_ids,
    basis_in,
    basis_out,
    leaf_up,
    leaf_down,
    leaf_coupling,
    leaf_far,
    leaf_count,
    cluster_up,
    cluster_down,
    cluster_coupling,
    cluster_far,
    group_up,
    group_down,
    group_coupling,
    group_far,
    root_coupling,
):
    wide = jnp.float32
    narrow = jnp.bfloat16
    leaves = densities.shape[0]
    coeff_order = basis_in.shape[1]
    columns = densities.shape[1]
    flat = coeff_order * columns
    first_leaf = lax.axis_index(("gx", "gy")) * leaves
    gx_index = lax.axis_index("gx")
    group_size = lax.axis_size("gy")
    groups = lax.axis_size("gx")
    leaf_coeffs = jnp.einsum(
        "lkm,lrm->lkr", basis_in, densities, preferred_element_type=wide
    ).astype(narrow)
    mid_coeffs = jnp.einsum(
        "lik,lkr->ir", leaf_up, leaf_coeffs, preferred_element_type=wide
    ).astype(narrow)
    mid_term = jnp.dot(cluster_up[0], mid_coeffs, preferred_element_type=wide).reshape(1, flat)
    mid_flat = mid_coeffs.reshape(1, flat)
    siblings = lax.all_gather(mid_flat, "gy", axis=0, tiled=True)
    group_sum = lax.psum(mid_term, "gy")
    nearby = padded(siblings, (("gx", 0),), group_size)
    mid_picked = jnp.take(nearby, cluster_far[0] - (gx_index - 1) * group_size, axis=0)
    top_coeffs = lax.all_gather(group_sum.astype(narrow), "gx", axis=0, tiled=True)
    top_block = top_coeffs.reshape(groups, coeff_order, columns)
    root_terms = jnp.einsum("gik,gkr->gir", group_up, top_block, preferred_element_type=wide)
    root_coeffs = jnp.sum(
        root_terms.reshape(groups // BRANCH, BRANCH, coeff_order, columns), axis=1
    ).astype(narrow)
    root_row = lax.dynamic_index_in_dim(root_coupling, gx_index // BRANCH, 0, keepdims=False)
    root_field = jnp.einsum(
        "sik,skr->ir", root_row, root_coeffs, preferred_element_type=wide
    ).astype(narrow)
    top_picked = jnp.take(top_block, group_far[0], axis=0)
    top_field = (
        jnp.einsum("fik,fkr->ir", group_coupling[0], top_picked, preferred_element_type=wide)
        + jnp.dot(group_down[0], root_field, preferred_element_type=wide)
    ).astype(narrow)
    mid_block = mid_picked.reshape(-1, coeff_order, columns)
    mid_field = (
        jnp.einsum("fik,fkr->ir", cluster_coupling[0], mid_block, preferred_element_type=wide)
        + jnp.dot(cluster_down[0], top_field, preferred_element_type=wide)
    ).astype(narrow)
    coeff_rim = padded(leaf_coeffs.reshape(leaves, flat), ((("gx", "gy"), 0),), leaves)
    picked = jnp.take(coeff_rim, leaf_far - (first_leaf - leaves), axis=0).reshape(
        leaves, -1, coeff_order, columns
    )
    live_mask = (lax.broadcasted_iota(jnp.int32, leaf_far.shape, 1) < leaf_count[:, None]).astype(
        narrow
    )
    picked = picked * live_mask[:, :, None, None]
    leaf_field = (
        jnp.einsum("lfik,lfkr->lir", leaf_coupling, picked, preferred_element_type=wide)
        + jnp.einsum("lik,kr->lir", leaf_down, mid_field, preferred_element_type=wide)
    ).astype(narrow)
    far_part = jnp.einsum("lkr,lkm->lrm", leaf_field, basis_out, preferred_element_type=wide)
    values_rim = padded(densities, ((("gx", "gy"), 0),), REACH)
    shape_rim = padded(geometry, ((("gx", "gy"), 0),), REACH)
    near_local = near_ids - (first_leaf - REACH)

    def near_block(pieces):
        target, indices = pieces
        source = jnp.take(shape_rim, indices, axis=0)
        values = jnp.take(values_rim, indices, axis=0)
        kernel = near_kernel(target, source).astype(narrow)
        return jnp.einsum("bmnj,bnrj->brm", kernel, values, preferred_element_type=wide)

    near_part = lax.map(
        near_block,
        (
            geometry.reshape(leaves // leaf_block, leaf_block, 7, -1),
            near_local.reshape(leaves // leaf_block, leaf_block, -1),
        ),
    )
    return far_part + near_part.reshape(far_part.shape)


def solution(mesh):
    return jax.shard_map(
        on_device,
        mesh=mesh,
        in_specs=(
            P(("gx", "gy"), None, None),
            P(("gx", "gy"), None, None),
            P(("gx", "gy"), None),
            P(("gx", "gy"), None, None),
            P(("gx", "gy"), None, None),
            P(("gx", "gy"), None, None),
            P(("gx", "gy"), None, None),
            P(("gx", "gy"), None, None, None),
            P(("gx", "gy"), None),
            P(("gx", "gy")),
            P(("gx", "gy"), None, None),
            P(("gx", "gy"), None, None),
            P(("gx", "gy"), None, None, None),
            P(("gx", "gy"), None),
            P(),
            P("gx", None, None),
            P("gx", None, None, None),
            P("gx", None),
            P(),
        ),
        out_specs=P(("gx", "gy"), None, None),
        check_vma=False,
    )
```

profile of v0, /device:TPU:8, one launch (start us, length us, event | category | flops | bytes accessed | tf_op | source)
XLA Modules:
  0.0 328.0 jit_solution(2928487035204301218)
XLA Ops:
  0.0 2.6 convolution_convert_fusion
  4.9 9.3 %collective-permute-start.1 = (bf16[96,2048]{1,0:T(8,128)(2,1)}, bf16[96,2048]{1,0:T(8,128)(2,1)}, u32[]{:S(2)}, u32[]{:S(2)}) collective-permute-start(bf16[96,2048]{1,0:T(8,128)(2,1)} %copy.66), channel_id=1, source_target_pairs={{1,0},{2,1},{3,2},{4,3},{5,4},{6,5},{7,6},{8,7},{9,8},{10,9},{11,1... | collective-permute-start | bytes 1179656 | tf_op jit(solution)/shard_map/ppermute | solution.py:23
  14.2 1.9 collective-permute-start
  17.4 1.9 collective-permute-start.6
  19.3 8.0 %collective-permute-start.7 = (f32[4,7,128]{2,1,0:T(8,128)S(1)}, f32[4,7,128]{2,1,0:T(8,128)S(1)}, u32[]{:S(2)}, u32[]{:S(2)}) collective-permute-start(f32[4,7,128]{2,1,0:T(8,128)S(1)} %get-tuple-element.83), channel_id=1, source_target_pairs={{1,0},{2,1},{3,2},{4,3},{5,4},{6,5},{7,6},{8,7},{9,8},{10,9},{11,1... | collective-permute-start | bytes 43016 | tf_op jit(solution)/shard_map/ppermute | solution.py:23
  27.3 4.0 %copy.72 = bf16[96,64,64]{2,1,0:T(8,128)(2,1)} copy(bf16[96,64,64]{0,2,1:T(8,128)(2,1)} %param.26) | data formatting | bytes 1572864 | tf_op args[5]
  31.4 2.0 fusion.35
  33.5 12.8 %all-gather = bf16[8,1,2048]{2,1,0:T(2,128)(2,1)S(1)} all-gather(bf16[1,1,2048]{2,1,0:T(2,128)(2,1)S(1)} %reshape.240), channel_id=1, replica_groups=mesh['gx'=32,'gy'=8] {'gy'}, dimensions={0}, use_global_device_ids=true | all-gather | bytes 36864 | tf_op jit(solution)/shard_map/all_gather | solution.py:85
  50.4 24.5 %psum.7 = bf16[1,2048]{1,0:T(2,128)(2,1)S(1)} all-reduce(f32[1,2048]{1,0:T(1,128)S(1)} %reshape.189), channel_id=1, replica_groups=mesh['gx'=32,'gy'=8] {'gy'}, use_global_device_ids=true, to_apply=%region_0.0 | all-reduce | flops 2048 | bytes 12288 | tf_op jit(solution)/shard_map/psum | solution.py:86
  74.9 48.0 %all-gather.1 = bf16[32,1,2048]{2,1,0:T(2,128)(2,1)S(1)} all-gather(bf16[1,1,2048]{2,1,0:T(2,128)(2,1)S(1)} %bitcast.169), channel_id=1, replica_groups=mesh['gx'=32,'gy'=8] {'gx'}, dimensions={0}, use_global_device_ids=true | all-gather | bytes 135168 | tf_op jit(solution)/shard_map/all_gather | solution.py:89
  129.4 4.0 %copy.78 = bf16[96,64,64]{2,1,0:T(8,128)(2,1)} copy(bf16[96,64,64]{0,2,1:T(8,128)(2,1)} %param.27) | data formatting | bytes 1572864 | tf_op args[6]
  133.4 16.1 %copy.71 = bf16[96,6,64,64]{3,2,1,0:T(8,128)(2,1)} copy(bf16[96,6,64,64]{0,3,2,1:T(8,128)(2,1)} %param.28) | data formatting | bytes 9437184 | tf_op args[7]
  149.5 2.4 collective-permute-start.2
  152.0 1.9 collective-permute-start.4
  154.0 8.0 %collective-permute-start.5 = (bf16[4,32,128]{2,1,0:T(8,128)(2,1)S(1)}, bf16[4,32,128]{2,1,0:T(8,128)(2,1)S(1)}, u32[]{:S(2)}, u32[]{:S(2)}) collective-permute-start(bf16[4,32,128]{2,1,0:T(8,128)(2,1)S(1)} %get-tuple-element.81), channel_id=1, source_target_pairs={{1,0},{2,1},{3,2},{4,3},{5,4},{6,5},{7,6},{8,7},{9,8},{10,9},{11,1... | collective-permute-start | bytes 98312 | tf_op jit(solution)/shard_map/ppermute | solution.py:23
  164.7 130.7 %while.10 = (s32[]{:T(128)}, f32[12,8,32,128]{3,2,1,0:T(8,128)}, s32[12,8,8]{2,1,0:T(8,128)}, bf16[104,32,128]{2,1,0:T(8,128)(2,1)S(1)}, f32[104,7,128]{2,1,0:T(...) while((s32[]{:T(128)}, f32[12,8,32,128]{3,2,1,0:T(8,128)}, s32[12,8,8]{2,1,0:T(8,128)}, ...), condition=%wide.region_3.4_spmd, body=%wide.region_2.3_spmd.sunk | while | flops 87352896 | bytes 3410213 | solution.py:133
  169.7 5.9 %fusion.84 = f32[12,8,32,128]{3,2,1,0:T(8,128)} fusion(f32[12,8,32,128]{3,2,1,0:T(8,128)} %get-tuple-element.149, s32[]{:T(128)S(6)} %copy.97, f32[8,8,128]{2,1,0:T(8,128)S(1)} %bitcast.159, f32[8,128]{1,0:T(8,128)} %get-tuple-element.132, f32[8,8,128]{2,1,0:T(8,128)S(1)} %bitcast.160, f32[8,8,128]{2,1,0:T(8,128)S(1)} %bitcast.161, ...), kind=kOutput, calls=%fused_computation.21.clone.1 | convolution fusion | flops 87293952 | bytes 897092 | tf_op jit(solution)/shard_map/while/body/eval_jaxpr/bmnj,bnrj->brm/dot_general | solution.py:131
  180.6 5.9 %fusion.84 = f32[12,8,32,128]{3,2,1,0:T(8,128)} fusion(f32[12,8,32,128]{3,2,1,0:T(8,128)} %get-tuple-element.149, s32[]{:T(128)S(6)} %copy.97, f32[8,8,128]{2,1,0:T(8,128)S(1)} %bitcast.159, f32[8,128]{1,0:T(8,128)} %get-tuple-element.132, f32[8,8,128]{2,1,0:T(8,128)S(1)} %bitcast.160, f32[8,8,128]{2,1,0:T(8,128)S(1)} %bitcast.161, ...), kind=kOutput, calls=%fused_computation.21.clone.1 | convolution fusion | flops 87293952 | bytes 897092 | tf_op jit(solution)/shard_map/while/body/eval_jaxpr/bmnj,bnrj->brm/dot_general | solution.py:131
  191.5 5.9 %fusion.84 = f32[12,8,32,128]{3,2,1,0:T(8,128)} fusion(f32[12,8,32,128]{3,2,1,0:T(8,128)} %get-tuple-element.149, s32[]{:T(128)S(6)} %copy.97, f32[8,8,128]{2,1,0:T(8,128)S(1)} %bitcast.159, f32[8,128]{1,0:T(8,128)} %get-tuple-element.132, f32[8,8,128]{2,1,0:T(8,128)S(1)} %bitcast.160, f32[8,8,128]{2,1,0:T(8,128)S(1)} %bitcast.161, ...), kind=kOutput, calls=%fused_computation.21.clone.1 | convolution fusion | flops 87293952 | bytes 897092 | tf_op jit(solution)/shard_map/while/body/eval_jaxpr/bmnj,bnrj->brm/dot_general | solution.py:131
  202.4 5.9 %fusion.84 = f32[12,8,32,128]{3,2,1,0:T(8,128)} fusion(f32[12,8,32,128]{3,2,1,0:T(8,128)} %get-tuple-element.149, s32[]{:T(128)S(6)} %copy.97, f32[8,8,128]{2,1,0:T(8,128)S(1)} %bitcast.159, f32[8,128]{1,0:T(8,128)} %get-tuple-element.132, f32[8,8,128]{2,1,0:T(8,128)S(1)} %bitcast.160, f32[8,8,128]{2,1,0:T(8,128)S(1)} %bitcast.161, ...), kind=kOutput, calls=%fused_computation.21.clone.1 | convolution fusion | flops 87293952 | bytes 897092 | tf_op jit(solution)/shard_map/while/body/eval_jaxpr/bmnj,bnrj->brm/dot_general | solution.py:131
  213.3 5.9 %fusion.84 = f32[12,8,32,128]{3,2,1,0:T(8,128)} fusion(f32[12,8,32,128]{3,2,1,0:T(8,128)} %get-tuple-element.149, s32[]{:T(128)S(6)} %copy.97, f32[8,8,128]{2,1,0:T(8,128)S(1)} %bitcast.159, f32[8,128]{1,0:T(8,128)} %get-tuple-element.132, f32[8,8,128]{2,1,0:T(8,128)S(1)} %bitcast.160, f32[8,8,128]{2,1,0:T(8,128)S(1)} %bitcast.161, ...), kind=kOutput, calls=%fused_computation.21.clone.1 | convolution fusion | flops 87293952 | bytes 897092 | tf_op jit(solution)/shard_map/while/body/eval_jaxpr/bmnj,bnrj->brm/dot_general | solution.py:131
  224.2 5.9 %fusion.84 = f32[12,8,32,128]{3,2,1,0:T(8,128)} fusion(f32[12,8,32,128]{3,2,1,0:T(8,128)} %get-tuple-element.149, s32[]{:T(128)S(6)} %copy.97, f32[8,8,128]{2,1,0:T(8,128)S(1)} %bitcast.159, f32[8,128]{1,0:T(8,128)} %get-tuple-element.132, f32[8,8,128]{2,1,0:T(8,128)S(1)} %bitcast.160, f32[8,8,128]{2,1,0:T(8,128)S(1)} %bitcast.161, ...), kind=kOutput, calls=%fused_computation.21.clone.1 | convolution fusion | flops 87293952 | bytes 897092 | tf_op jit(solution)/shard_map/while/body/eval_jaxpr/bmnj,bnrj->brm/dot_general | solution.py:131
  235.1 5.9 %fusion.84 = f32[12,8,32,128]{3,2,1,0:T(8,128)} fusion(f32[12,8,32,128]{3,2,1,0:T(8,128)} %get-tuple-element.149, s32[]{:T(128)S(6)} %copy.97, f32[8,8,128]{2,1,0:T(8,128)S(1)} %bitcast.159, f32[8,128]{1,0:T(8,128)} %get-tuple-element.132, f32[8,8,128]{2,1,0:T(8,128)S(1)} %bitcast.160, f32[8,8,128]{2,1,0:T(8,128)S(1)} %bitcast.161, ...), kind=kOutput, calls=%fused_computation.21.clone.1 | convolution fusion | flops 87293952 | bytes 897092 | tf_op jit(solution)/shard_map/while/body/eval_jaxpr/bmnj,bnrj->brm/dot_general | solution.py:131
  246.0 5.9 %fusion.84 = f32[12,8,32,128]{3,2,1,0:T(8,128)} fusion(f32[12,8,32,128]{3,2,1,0:T(8,128)} %get-tuple-element.149, s32[]{:T(128)S(6)} %copy.97, f32[8,8,128]{2,1,0:T(8,128)S(1)} %bitcast.159, f32[8,128]{1,0:T(8,128)} %get-tuple-element.132, f32[8,8,128]{2,1,0:T(8,128)S(1)} %bitcast.160, f32[8,8,128]{2,1,0:T(8,128)S(1)} %bitcast.161, ...), kind=kOutput, calls=%fused_computation.21.clone.1 | convolution fusion | flops 87293952 | bytes 897092 | tf_op jit(solution)/shard_map/while/body/eval_jaxpr/bmnj,bnrj->brm/dot_general | solution.py:131
  256.9 5.9 %fusion.84 = f32[12,8,32,128]{3,2,1,0:T(8,128)} fusion(f32[12,8,32,128]{3,2,1,0:T(8,128)} %get-tuple-element.149, s32[]{:T(128)S(6)} %copy.97, f32[8,8,128]{2,1,0:T(8,128)S(1)} %bitcast.159, f32[8,128]{1,0:T(8,128)} %get-tuple-element.132, f32[8,8,128]{2,1,0:T(8,128)S(1)} %bitcast.160, f32[8,8,128]{2,1,0:T(8,128)S(1)} %bitcast.161, ...), kind=kOutput, calls=%fused_computation.21.clone.1 | convolution fusion | flops 87293952 | bytes 897092 | tf_op jit(solution)/shard_map/while/body/eval_jaxpr/bmnj,bnrj->brm/dot_general | solution.py:131
  267.8 5.9 %fusion.84 = f32[12,8,32,128]{3,2,1,0:T(8,128)} fusion(f32[12,8,32,128]{3,2,1,0:T(8,128)} %get-tuple-element.149, s32[]{:T(128)S(6)} %copy.97, f32[8,8,128]{2,1,0:T(8,128)S(1)} %bitcast.159, f32[8,128]{1,0:T(8,128)} %get-tuple-element.132, f32[8,8,128]{2,1,0:T(8,128)S(1)} %bitcast.160, f32[8,8,128]{2,1,0:T(8,128)S(1)} %bitcast.161, ...), kind=kOutput, calls=%fused_computation.21.clone.1 | convolution fusion | flops 87293952 | bytes 897092 | tf_op jit(solution)/shard_map/while/body/eval_jaxpr/bmnj,bnrj->brm/dot_general | solution.py:131
  278.7 5.9 %fusion.84 = f32[12,8,32,128]{3,2,1,0:T(8,128)} fusion(f32[12,8,32,128]{3,2,1,0:T(8,128)} %get-tuple-element.149, s32[]{:T(128)S(6)} %copy.97, f32[8,8,128]{2,1,0:T(8,128)S(1)} %bitcast.159, f32[8,128]{1,0:T(8,128)} %get-tuple-element.132, f32[8,8,128]{2,1,0:T(8,128)S(1)} %bitcast.160, f32[8,8,128]{2,1,0:T(8,128)S(1)} %bitcast.161, ...), kind=kOutput, calls=%fused_computation.21.clone.1 | convolution fusion | flops 87293952 | bytes 897092 | tf_op jit(solution)/shard_map/while/body/eval_jaxpr/bmnj,bnrj->brm/dot_general | solution.py:131
  289.6 5.9 %fusion.84 = f32[12,8,32,128]{3,2,1,0:T(8,128)} fusion(f32[12,8,32,128]{3,2,1,0:T(8,128)} %get-tuple-element.149, s32[]{:T(128)S(6)} %copy.97, f32[8,8,128]{2,1,0:T(8,128)S(1)} %bitcast.159, f32[8,128]{1,0:T(8,128)} %get-tuple-element.132, f32[8,8,128]{2,1,0:T(8,128)S(1)} %bitcast.160, f32[8,8,128]{2,1,0:T(8,128)S(1)} %bitcast.161, ...), kind=kOutput, calls=%fused_computation.21.clone.1 | convolution fusion | flops 87293952 | bytes 897092 | tf_op jit(solution)/shard_map/while/body/eval_jaxpr/bmnj,bnrj->brm/dot_general | solution.py:131
  296.5 4.3 %fusion.37 = f32[32,96,64]{2,0,1:T(8,128)} fusion(bf16[96,64,64]{2,1,0:T(8,128)(2,1)} %copy.78, f32[32,64]{1,0:T(8,128)S(1)} %convolution_bitcast_fusion.3, bf16[32,64]{1,0:T(8,128)(2,1)} %fusion.33, bf16[1,64,64]{2,1,0:T(8,128)(2,1)} %param.32), kind=kOutput, calls=%fused_computation.60 | convolution fusion | flops 25432064 | bytes 1593344 | tf_op jit(solution)/shard_map/lik,kr->lir/dot_general | solution.py:119
  302.1 4.0 %gather_fusion.2 = bf16[576,2048]{1,0:T(8,128)(2,1)} fusion(bf16[288,2048]{1,0:T(8,128)(2,1)S(1)} %pad_maximum_fusion, s32[1024]{0:T(1024)S(1)} %pad_clamp_fusion.3), kind=kCustom, calls=%fused_computation.2 | custom fusion | bytes 4720896 | tf_op jit(solution)/shard_map/jit(_take)/gather | solution.py:110
  306.1 11.7 %gather.23 = bf16[96,6,64,32]{3,2,1,0:T(8,128)(2,1)} reshape(bf16[576,2048]{1,0:T(8,128)(2,1)} %gather_fusion.2) | data formatting | bytes 4718592 | tf_op jit(solution)/shard_map/jit(_take)/gather | solution.py:110
  317.8 10.3 %bitcast_add_fusion.1 = f32[96,32,128]{2,1,0:T(8,128)} fusion(f32[12,8,32,128]{3,2,1,0:T(8,128)} %get-tuple-element.37, bf16[96,64,128]{2,1,0:T(8,128)(2,1)S(1)} %copy-done, f32[32,96,64]{2,0,1:T(8,128)S(1)} %copy-done.1, bf16[96,6,64,64]{3,2,1,0:T(8,128)(2,1)} %copy.71, bf16[96,6,64,32]{3,2,1,0:T(8,128)(2,1)} %gather.23, pred[96,6]{1,0:T(8,128)(4,1)S(1)} %copy-done.6, ...), kind=kOutput, calls=%fused_computation.44 | convolution fusion | flops 204472320 | bytes 12584640 | tf_op jit(solution)/shard_map/lkr,lkm->lrm/dot_general | solution.py:121
  (193 shorter events, 79.2 us)
Async XLA Ops:
  0.0 317.8 %copy-start = (bf16[96,64,128]{2,1,0:T(8,128)(2,1)S(1)}, bf16[96,64,128]{2,1,0:T(8,128)(2,1)}, u32[]{:S(2)}) copy-start(bf16[96,64,128]{2,1,0:T(8,128)(2,1)} %param.25) | copy-start | bytes 4718596
  4.9 295.9 %collective-permute-start.1 = (bf16[96,2048]{1,0:T(8,128)(2,1)}, bf16[96,2048]{1,0:T(8,128)(2,1)}, u32[]{:S(2)}, u32[]{:S(2)}) collective-permute-start(bf16[96,2048]{1,0:T(8,128)(2,1)} %copy.66), channel_id=1, source_target_pairs={{1,0},{2,1},{3,2},{4,3},{5,4},{6,5},{7,6},{8,7},{9,8},{10,9},{11,1... | collective-permute-start | bytes 1179656 | tf_op jit(solution)/shard_map/ppermute | solution.py:23
  14.2 286.6 %collective-permute-start = (bf16[96,2048]{1,0:T(8,128)(2,1)}, bf16[96,2048]{1,0:T(8,128)(2,1)}, u32[]{:S(2)}, u32[]{:S(2)}) collective-permute-start(bf16[96,2048]{1,0:T(8,128)(2,1)} %copy.66), channel_id=1, source_target_pairs={{0,1},{1,2},{2,3},{3,4},{4,5},{5,6},{6,7},{7,8},{8,9},{9,10},{10,1... | collective-permute-start | bytes 1179656 | tf_op jit(solution)/shard_map/ppermute | solution.py:21
  17.4 132.2 %collective-permute-start.6 = (f32[4,7,128]{2,1,0:T(8,128)S(1)}, f32[4,7,128]{2,1,0:T(8,128)S(1)}, u32[]{:S(2)}, u32[]{:S(2)}) collective-permute-start(f32[4,7,128]{2,1,0:T(8,128)S(1)} %get-tuple-element.82), channel_id=1, source_target_pairs={{0,1},{1,2},{2,3},{3,4},{4,5},{5,6},{6,7},{7,8},{8,9},{9,10},{10,1... | collective-permute-start | bytes 43016 | tf_op jit(solution)/shard_map/ppermute | solution.py:21
  19.3 29.0 %copy-start.10 = (s32[1,6]{1,0:T(1,128)S(1)}, s32[1,6]{1,0:T(1,128)}, u32[]{:S(2)}) copy-start(s32[1,6]{1,0:T(1,128)} %param.34) | copy-start | bytes 76
  19.3 29.0 %copy-start.11 = (s32[1,6]{1,0:T(1,128)S(1)}, s32[1,6]{1,0:T(1,128)}, u32[]{:S(2)}) copy-start(s32[1,6]{1,0:T(1,128)} %param.38) | copy-start | bytes 76
  19.3 29.8 %copy-start.9 = (s32[96]{0:T(128)S(1)}, s32[96]{0:T(128)}, u32[]{:S(2)}) copy-start(s32[96]{0:T(128)} %param.30) | copy-start | bytes 1156
  19.3 30.5 %copy-start.7 = (s32[96,6]{0,1:T(8,128)S(1)}, s32[96,6]{0,1:T(8,128)}, u32[]{:S(2)}) copy-start(s32[96,6]{0,1:T(8,128)} %param.29) | copy-start | bytes 6916
  19.3 30.8 %copy-start.4 = (bf16[1,64,64]{2,1,0:T(8,128)(2,1)S(1)}, bf16[1,64,64]{2,1,0:T(8,128)(2,1)}, u32[]{:S(2)}) copy-start(bf16[1,64,64]{2,1,0:T(8,128)(2,1)} %param.31) | copy-start | bytes 24580
  19.3 132.6 %collective-permute-start.7 = (f32[4,7,128]{2,1,0:T(8,128)S(1)}, f32[4,7,128]{2,1,0:T(8,128)S(1)}, u32[]{:S(2)}, u32[]{:S(2)}) collective-permute-start(f32[4,7,128]{2,1,0:T(8,128)S(1)} %get-tuple-element.83), channel_id=1, source_target_pairs={{1,0},{2,1},{3,2},{4,3},{5,4},{6,5},{7,6},{8,7},{9,8},{10,9},{11,1... | collective-permute-start | bytes 43016 | tf_op jit(solution)/shard_map/ppermute | solution.py:23
  31.4 92.7 %copy-start.2 = (bf16[32,64,64]{2,1,0:T(8,128)(2,1)S(1)}, bf16[32,64,64]{2,1,0:T(8,128)(2,1)}, u32[]{:S(2)}) copy-start(bf16[32,64,64]{2,1,0:T(8,128)(2,1)} %param.35) | copy-start | bytes 786436
  31.4 93.7 %copy-start.8 = (s32[96,8]{0,1:T(8,128)S(1)}, s32[96,8]{0,1:T(8,128)}, u32[]{:S(2)}) copy-start(s32[96,8]{0,1:T(8,128)} %param.23) | copy-start | bytes 9220
  33.3 92.9 %copy-start.5 = (bf16[1,64,64]{2,1,0:T(8,128)(2,1)S(1)}, bf16[1,64,64]{2,1,0:T(8,128)(2,1)}, u32[]{:S(2)}) copy-start(bf16[1,64,64]{2,1,0:T(8,128)(2,1)} %param.36) | copy-start | bytes 24580
  46.3 107.6 %collective-permute-start.3 = (bf16[8,2048]{1,0:T(8,128)(2,1)S(1)}, bf16[8,2048]{1,0:T(8,128)(2,1)S(1)}, u32[]{:S(2)}, u32[]{:S(2)}) collective-permute-start(bf16[8,2048]{1,0:T(8,128)(2,1)S(1)} %bitcast.165), channel_id=1, source_target_pairs={{8,0},{16,8},{24,16},{32,24},{40,32},{48,40},{56,48},{64,56},{72,6... | collective-permute-start | bytes 98312 | tf_op jit(solution)/shard_map/ppermute | solution.py:23
  149.5 12.5 %collective-permute-start.2 = (bf16[8,2048]{1,0:T(8,128)(2,1)S(1)}, bf16[8,2048]{1,0:T(8,128)(2,1)S(1)}, u32[]{:S(2)}, u32[]{:S(2)}) collective-permute-start(bf16[8,2048]{1,0:T(8,128)(2,1)S(1)} %bitcast.166), channel_id=1, source_target_pairs={{0,8},{8,16},{16,24},{24,32},{32,40},{40,48},{48,56},{56,64},{64,7... | collective-permute-start | bytes 98312 | tf_op jit(solution)/shard_map/ppermute | solution.py:21
  152.0 11.5 %collective-permute-start.4 = (bf16[4,32,128]{2,1,0:T(8,128)(2,1)S(1)}, bf16[4,32,128]{2,1,0:T(8,128)(2,1)S(1)}, u32[]{:S(2)}, u32[]{:S(2)}) collective-permute-start(bf16[4,32,128]{2,1,0:T(8,128)(2,1)S(1)} %get-tuple-element.80), channel_id=1, source_target_pairs={{0,1},{1,2},{2,3},{3,4},{4,5},{5,6},{6,7},{7,8},{8,9},{9,10},{10,1... | collective-permute-start | bytes 98312 | tf_op jit(solution)/shard_map/ppermute | solution.py:21
  154.0 9.5 %collective-permute-start.5 = (bf16[4,32,128]{2,1,0:T(8,128)(2,1)S(1)}, bf16[4,32,128]{2,1,0:T(8,128)(2,1)S(1)}, u32[]{:S(2)}, u32[]{:S(2)}) collective-permute-start(bf16[4,32,128]{2,1,0:T(8,128)(2,1)S(1)} %get-tuple-element.81), channel_id=1, source_target_pairs={{1,0},{2,1},{3,2},{4,3},{5,4},{6,5},{7,6},{8,7},{9,8},{10,9},{11,1... | collective-permute-start | bytes 98312 | tf_op jit(solution)/shard_map/ppermute | solution.py:23
  306.1 11.7 %copy-start.1 = (f32[32,96,64]{2,0,1:T(8,128)S(1)}, f32[32,96,64]{2,0,1:T(8,128)}, u32[]{:S(2)}) copy-start(f32[32,96,64]{2,0,1:T(8,128)} %fusion.37) | copy-start | bytes 2359300
  306.1 11.7 %copy-start.3 = (bf16[96,6]{1,0:T(8,128)(2,1)S(1)}, bf16[96,6]{1,0:T(8,128)(2,1)}, u32[]{:S(2)}) copy-start(bf16[96,6]{1,0:T(8,128)(2,1)} %fusion.49) | copy-start | bytes 3460
  306.1 11.7 %copy-start.6 = (pred[96,6]{1,0:T(8,128)(4,1)S(1)}, pred[96,6]{1,0:T(8,128)(4,1)}, u32[]{:S(2)}) copy-start(pred[96,6]{1,0:T(8,128)(4,1)} %copy.64) | copy-start | bytes 1732
where the time goes:
time: 331 us; the launch traced here: 328 us
  matrix products  94.2 us (28%)
  local copies, waits for them, and re-layouts  90.2 us (27%)
  blocking collectives  85.2 us (26%)
  starting transfers between devices  35.4 us (11%)
  other arithmetic  22.2 us (7%)
    dot_general x12, matrix products, near_block(): jnp.einsum('bmnj,bnrj->brm', kernel, values, preferred_element_type=wide)  70.5 us
    all_gather x1, blocking collectives, on_device(): lax.all_gather(group_sum.astype(narrow), 'gx', axis=0, tiled=True)  48 us
    ppermute x4, starting transfers between devices, padded(): lax.ppermute(head, axis, [((i + 1) % count, i) for i in range(ends)])  27.2 us
    unnamed x30, local copies, waits for them, and re-layouts  25.5 us
    psum x1, blocking collectives, on_device(): group_sum = lax.psum(mid_term, 'gy')  24.5 us
    gather x2, local copies, waits for them, and re-layouts, on_device(): jnp.take(coeff_rim, leaf_far - (first_leaf - leaves), axis=0)  15.6 us
    all_gather x1, blocking collectives, on_device(): siblings = lax.all_gather(mid_flat, 'gy', axis=0, tiled=True)  12.8 us
    dot_general x1, matrix products, on_device(): jnp.einsum('lkr,lkm->lrm', leaf_field, basis_out, preferred_element_type=...  10.3 us
  transfers between devices with their start and end apart: 8, of which 0 were waited for; matrix products, arithmetic and copies ran while one was open for 53% of the time, Pallas kernels for 0%

commit v1 on v0

--- a/solution.py
+++ b/solution.py
@@ -8,6 +8,12 @@
 BRANCH = 4
 four_pi = 4.0 * math.pi
 leaf_block = 8
+
+
+def gather_from_all(x, axis, dim):
+    size = lax.axis_size(axis)
+    repeats = [size if d == dim else 1 for d in range(x.ndim)]
+    return lax.all_to_all(jnp.tile(x, repeats), axis, split_axis=dim, concat_axis=dim, tiled=True)
 
 
 def padded(cells, sides, width):
@@ -86,7 +92,7 @@
     group_sum = lax.psum(mid_term, "gy")
     nearby = padded(siblings, (("gx", 0),), group_size)
     mid_picked = jnp.take(nearby, cluster_far[0] - (gx_index - 1) * group_size, axis=0)
-    top_coeffs = lax.all_gather(group_sum.astype(narrow), "gx", axis=0, tiled=True)
+    top_coeffs = gather_from_all(group_sum.astype(narrow), "gx", 0)
     top_block = top_coeffs.reshape(groups, coeff_order, columns)
     root_terms = jnp.einsum("gik,gkr->gir", group_up, top_block, preferred_element_type=wide)
     root_coeffs = jnp.sum(

time: 331 us -> 296 us (0.89)
  blocking collectives: 85.2 us -> 36.7 us
  other arithmetic: 22.2 us -> 27.5 us
  local copies, waits for them, and re-layouts: 90.2 us -> 95 us
    all_gather x1 -> x0, blocking collectives: 48 us -> none  [on_device(): lax.all_gather(group_sum.astype(narrow), 'gx', axis=0, tiled=True)]
    all_to_all x0 -> x1, starting transfers between devices: none -> 5.65 us  [gather_from_all(): lax.all_to_all(jnp.tile(x, repeats), axis, split_axis=dim, concat_axis=di...]
    unnamed x30 -> x36, local copies, waits for them, and re-layouts: 25.5 us -> 28.2 us
  transfers between devices with their start and end apart: 8 -> 9, of which waited for: 0 -> 0; matrix products, arithmetic and copies ran while one was open for 53% -> 63% of each run, Pallas kernels for 0% -> 0%
where the time goes in v1:
time: 296 us; the launch traced here: 292 us
  local copies, waits for them, and re-layouts  95 us (32%)
  matrix products  94 us (32%)
  starting transfers between devices  38.5 us (13%)
  blocking collectives  36.7 us (12%)
  other arithmetic  27.5 us (9%)
    dot_general x12, matrix products, near_block(): jnp.einsum('bmnj,bnrj->brm', kernel, values, preferred_element_type=wide)  70.5 us
    unnamed x36, local copies, waits for them, and re-layouts  28.2 us
    ppermute x4, starting transfers between devices, padded(): lax.ppermute(head, axis, [((i + 1) % count, i) for i in range(ends)])  24.5 us
    psum x1, blocking collectives, on_device(): group_sum = lax.psum(mid_term, 'gy')  23.9 us
    gather x2, local copies, waits for them, and re-layouts, on_device(): jnp.take(coeff_rim, leaf_far - (first_leaf - leaves), axis=0)  15.6 us
    all_gather x1, blocking collectives, on_device(): siblings = lax.all_gather(mid_flat, 'gy', axis=0, tiled=True)  12.8 us
    dot_general x1, matrix products, on_device(): jnp.einsum('lkr,lkm->lrm', leaf_field, basis_out, preferred_element_type=...  10.3 us
    slice x12, local copies, waits for them, and re-layouts, near_kernel(): panel_area = source[:, None, :, 6, :]  9.31 us
  transfers between devices with their start and end apart: 9, of which 0 were waited for; matrix products, arithmetic and copies ran while one was open for 63% of the time, Pallas kernels for 0%

profile of v1, /device:TPU:8, one launch (start us, length us, event | category | flops | bytes accessed | tf_op | source)
XLA Modules:
  0.0 292.4 jit_solution(941053071900236881)
XLA Ops:
  0.0 2.6 convolution_convert_fusion
  4.9 9.3 %collective-permute-start.1 = (bf16[96,2048]{1,0:T(8,128)(2,1)}, bf16[96,2048]{1,0:T(8,128)(2,1)}, u32[]{:S(2)}, u32[]{:S(2)}) collective-permute-start(bf16[96,2048]{1,0:T(8,128)(2,1)} %copy.66), channel_id=1, source_target_pairs={{1,0},{2,1},{3,2},{4,3},{5,4},{6,5},{7,6},{8,7},{9,8},{10,9},{11,1... | collective-permute-start | bytes 1179656 | tf_op jit(solution)/shard_map/ppermute | solution.py:29
  14.2 1.9 collective-permute-start
  20.0 1.9 collective-permute-start.6
  22.0 7.9 %collective-permute-start.7 = (f32[4,7,128]{2,1,0:T(8,128)S(1)}, f32[4,7,128]{2,1,0:T(8,128)S(1)}, u32[]{:S(2)}, u32[]{:S(2)}) collective-permute-start(f32[4,7,128]{2,1,0:T(8,128)S(1)} %get-tuple-element.83), channel_id=1, source_target_pairs={{1,0},{2,1},{3,2},{4,3},{5,4},{6,5},{7,6},{8,7},{9,8},{10,9},{11,1... | collective-permute-start | bytes 43016 | tf_op jit(solution)/shard_map/ppermute | solution.py:29
  29.8 4.0 %copy.72 = bf16[96,64,64]{2,1,0:T(8,128)(2,1)} copy(bf16[96,64,64]{0,2,1:T(8,128)(2,1)} %param.26) | data formatting | bytes 1572864 | tf_op args[5]
  33.9 2.0 fusion.35
  36.2 23.9 %psum.7 = bf16[1,2048]{1,0:T(2,128)(2,1)S(1)} all-reduce(f32[1,2048]{1,0:T(1,128)S(1)} %reshape.199), channel_id=1, replica_groups=mesh['gx'=32,'gy'=8] {'gy'}, use_global_device_ids=true, to_apply=%region_0.0 | all-reduce | flops 2048 | bytes 12288 | tf_op jit(solution)/shard_map/psum | solution.py:92
  62.9 5.6 %all-to-all-start = ((bf16[32,2,1024]{2,1,0:T(2,128)(2,1)}), bf16[32,2,1024]{2,1,0:T(2,128)(2,1)}, u32[]{:S(2)}, u32[]{:S(2)}) async-start(bf16[32,2,1024]{2,1,0:T(2,128)(2,1)} %reshape.262), calls=%async_computation | async-start | bytes 262144 | tf_op jit(solution)/shard_map/all_to_all | solution.py:16
  73.6 12.8 %all-gather = bf16[8,1,2048]{2,1,0:T(2,128)(2,1)S(1)} all-gather(bf16[1,1,2048]{2,1,0:T(2,128)(2,1)S(1)} %reshape.250), channel_id=1, replica_groups=mesh['gx'=32,'gy'=8] {'gy'}, dimensions={0}, use_global_device_ids=true | all-gather | bytes 36864 | tf_op jit(solution)/shard_map/all_gather | solution.py:91
  86.9 4.0 %copy.78 = bf16[96,64,64]{2,1,0:T(8,128)(2,1)} copy(bf16[96,64,64]{0,2,1:T(8,128)(2,1)} %param.27) | data formatting | bytes 1572864 | tf_op args[6]
  90.9 16.1 %copy.71 = bf16[96,6,64,64]{3,2,1,0:T(8,128)(2,1)} copy(bf16[96,6,64,64]{0,3,2,1:T(8,128)(2,1)} %param.28) | data formatting | bytes 9437184 | tf_op args[7]
  107.0 4.0 %collective-permute-start.5 = (bf16[4,32,128]{2,1,0:T(8,128)(2,1)S(1)}, bf16[4,32,128]{2,1,0:T(8,128)(2,1)S(1)}, u32[]{:S(2)}, u32[]{:S(2)}) collective-permute-start(bf16[4,32,128]{2,1,0:T(8,128)(2,1)S(1)} %get-tuple-element.81), channel_id=1, source_target_pairs={{1,0},{2,1},{3,2},{4,3},{5,4},{6,5},{7,6},{8,7},{9,8},{10,9},{11,1... | collective-permute-start | bytes 98312 | tf_op jit(solution)/shard_map/ppermute | solution.py:29
  111.0 3.4 %collective-permute-start.3 = (bf16[8,2048]{1,0:T(8,128)(2,1)}, bf16[8,2048]{1,0:T(8,128)(2,1)}, u32[]{:S(2)}, u32[]{:S(2)}) collective-permute-start(bf16[8,2048]{1,0:T(8,128)(2,1)} %bitcast.123), channel_id=1, source_target_pairs={{8,0},{16,8},{24,16},{32,24},{40,32},{48,40},{56,48},{64,56},{72,6... | collective-permute-start | bytes 98312 | tf_op jit(solution)/shard_map/ppermute | solution.py:29
  114.4 2.7 collective-permute-start.2
  118.4 130.7 %while.10 = (s32[]{:T(128)}, f32[12,8,32,128]{3,2,1,0:T(8,128)}, s32[12,8,8]{2,1,0:T(8,128)}, bf16[104,32,128]{2,1,0:T(8,128)(2,1)S(1)}, f32[104,7,128]{2,1,0:T(...) while((s32[]{:T(128)}, f32[12,8,32,128]{3,2,1,0:T(8,128)}, s32[12,8,8]{2,1,0:T(8,128)}, ...), condition=%wide.region_3.4_spmd, body=%wide.region_2.3_spmd.sunk | while | flops 87352896 | bytes 3410213 | solution.py:139
  123.4 5.9 %fusion.84 = f32[12,8,32,128]{3,2,1,0:T(8,128)} fusion(f32[12,8,32,128]{3,2,1,0:T(8,128)} %get-tuple-element.149, s32[]{:T(128)S(6)} %copy.97, f32[8,8,128]{2,1,0:T(8,128)S(1)} %bitcast.156, f32[8,128]{1,0:T(8,128)} %get-tuple-element.132, f32[8,8,128]{2,1,0:T(8,128)S(1)} %bitcast.157, f32[8,8,128]{2,1,0:T(8,128)S(1)} %bitcast.158, ...), kind=kOutput, calls=%fused_computation.21.clone.1 | convolution fusion | flops 87293952 | bytes 897092 | tf_op jit(solution)/shard_map/while/body/eval_jaxpr/bmnj,bnrj->brm/dot_general | solution.py:137
  134.3 5.9 %fusion.84 = f32[12,8,32,128]{3,2,1,0:T(8,128)} fusion(f32[12,8,32,128]{3,2,1,0:T(8,128)} %get-tuple-element.149, s32[]{:T(128)S(6)} %copy.97, f32[8,8,128]{2,1,0:T(8,128)S(1)} %bitcast.156, f32[8,128]{1,0:T(8,128)} %get-tuple-element.132, f32[8,8,128]{2,1,0:T(8,128)S(1)} %bitcast.157, f32[8,8,128]{2,1,0:T(8,128)S(1)} %bitcast.158, ...), kind=kOutput, calls=%fused_computation.21.clone.1 | convolution fusion | flops 87293952 | bytes 897092 | tf_op jit(solution)/shard_map/while/body/eval_jaxpr/bmnj,bnrj->brm/dot_general | solution.py:137
  145.2 5.9 %fusion.84 = f32[12,8,32,128]{3,2,1,0:T(8,128)} fusion(f32[12,8,32,128]{3,2,1,0:T(8,128)} %get-tuple-element.149, s32[]{:T(128)S(6)} %copy.97, f32[8,8,128]{2,1,0:T(8,128)S(1)} %bitcast.156, f32[8,128]{1,0:T(8,128)} %get-tuple-element.132, f32[8,8,128]{2,1,0:T(8,128)S(1)} %bitcast.157, f32[8,8,128]{2,1,0:T(8,128)S(1)} %bitcast.158, ...), kind=kOutput, calls=%fused_computation.21.clone.1 | convolution fusion | flops 87293952 | bytes 897092 | tf_op jit(solution)/shard_map/while/body/eval_jaxpr/bmnj,bnrj->brm/dot_general | solution.py:137
  156.1 5.9 %fusion.84 = f32[12,8,32,128]{3,2,1,0:T(8,128)} fusion(f32[12,8,32,128]{3,2,1,0:T(8,128)} %get-tuple-element.149, s32[]{:T(128)S(6)} %copy.97, f32[8,8,128]{2,1,0:T(8,128)S(1)} %bitcast.156, f32[8,128]{1,0:T(8,128)} %get-tuple-element.132, f32[8,8,128]{2,1,0:T(8,128)S(1)} %bitcast.157, f32[8,8,128]{2,1,0:T(8,128)S(1)} %bitcast.158, ...), kind=kOutput, calls=%fused_computation.21.clone.1 | convolution fusion | flops 87293952 | bytes 897092 | tf_op jit(solution)/shard_map/while/body/eval_jaxpr/bmnj,bnrj->brm/dot_general | solution.py:137
  167.0 5.9 %fusion.84 = f32[12,8,32,128]{3,2,1,0:T(8,128)} fusion(f32[12,8,32,128]{3,2,1,0:T(8,128)} %get-tuple-element.149, s32[]{:T(128)S(6)} %copy.97, f32[8,8,128]{2,1,0:T(8,128)S(1)} %bitcast.156, f32[8,128]{1,0:T(8,128)} %get-tuple-element.132, f32[8,8,128]{2,1,0:T(8,128)S(1)} %bitcast.157, f32[8,8,128]{2,1,0:T(8,128)S(1)} %bitcast.158, ...), kind=kOutput, calls=%fused_computation.21.clone.1 | convolution fusion | flops 87293952 | bytes 897092 | tf_op jit(solution)/shard_map/while/body/eval_jaxpr/bmnj,bnrj->brm/dot_general | solution.py:137
  177.8 5.9 %fusion.84 = f32[12,8,32,128]{3,2,1,0:T(8,128)} fusion(f32[12,8,32,128]{3,2,1,0:T(8,128)} %get-tuple-element.149, s32[]{:T(128)S(6)} %copy.97, f32[8,8,128]{2,1,0:T(8,128)S(1)} %bitcast.156, f32[8,128]{1,0:T(8,128)} %get-tuple-element.132, f32[8,8,128]{2,1,0:T(8,128)S(1)} %bitcast.157, f32[8,8,128]{2,1,0:T(8,128)S(1)} %bitcast.158, ...), kind=kOutput, calls=%fused_computation.21.clone.1 | convolution fusion | flops 87293952 | bytes 897092 | tf_op jit(solution)/shard_map/while/body/eval_jaxpr/bmnj,bnrj->brm/dot_general | solution.py:137
  188.7 5.9 %fusion.84 = f32[12,8,32,128]{3,2,1,0:T(8,128)} fusion(f32[12,8,32,128]{3,2,1,0:T(8,128)} %get-tuple-element.149, s32[]{:T(128)S(6)} %copy.97, f32[8,8,128]{2,1,0:T(8,128)S(1)} %bitcast.156, f32[8,128]{1,0:T(8,128)} %get-tuple-element.132, f32[8,8,128]{2,1,0:T(8,128)S(1)} %bitcast.157, f32[8,8,128]{2,1,0:T(8,128)S(1)} %bitcast.158, ...), kind=kOutput, calls=%fused_computation.21.clone.1 | convolution fusion | flops 87293952 | bytes 897092 | tf_op jit(solution)/shard_map/while/body/eval_jaxpr/bmnj,bnrj->brm/dot_general | solution.py:137
  199.6 5.9 %fusion.84 = f32[12,8,32,128]{3,2,1,0:T(8,128)} fusion(f32[12,8,32,128]{3,2,1,0:T(8,128)} %get-tuple-element.149, s32[]{:T(128)S(6)} %copy.97, f32[8,8,128]{2,1,0:T(8,128)S(1)} %bitcast.156, f32[8,128]{1,0:T(8,128)} %get-tuple-element.132, f32[8,8,128]{2,1,0:T(8,128)S(1)} %bitcast.157, f32[8,8,128]{2,1,0:T(8,128)S(1)} %bitcast.158, ...), kind=kOutput, calls=%fused_computation.21.clone.1 | convolution fusion | flops 87293952 | bytes 897092 | tf_op jit(solution)/shard_map/while/body/eval_jaxpr/bmnj,bnrj->brm/dot_general | solution.py:137
  210.5 5.9 %fusion.84 = f32[12,8,32,128]{3,2,1,0:T(8,128)} fusion(f32[12,8,32,128]{3,2,1,0:T(8,128)} %get-tuple-element.149, s32[]{:T(128)S(6)} %copy.97, f32[8,8,128]{2,1,0:T(8,128)S(1)} %bitcast.156, f32[8,128]{1,0:T(8,128)} %get-tuple-element.132, f32[8,8,128]{2,1,0:T(8,128)S(1)} %bitcast.157, f32[8,8,128]{2,1,0:T(8,128)S(1)} %bitcast.158, ...), kind=kOutput, calls=%fused_computation.21.clone.1 | convolution fusion | flops 87293952 | bytes 897092 | tf_op jit(solution)/shard_map/while/body/eval_jaxpr/bmnj,bnrj->brm/dot_general | solution.py:137
  221.4 5.9 %fusion.84 = f32[12,8,32,128]{3,2,1,0:T(8,128)} fusion(f32[12,8,32,128]{3,2,1,0:T(8,128)} %get-tuple-element.149, s32[]{:T(128)S(6)} %copy.97, f32[8,8,128]{2,1,0:T(8,128)S(1)} %bitcast.156, f32[8,128]{1,0:T(8,128)} %get-tuple-element.132, f32[8,8,128]{2,1,0:T(8,128)S(1)} %bitcast.157, f32[8,8,128]{2,1,0:T(8,128)S(1)} %bitcast.158, ...), kind=kOutput, calls=%fused_computation.21.clone.1 | convolution fusion | flops 87293952 | bytes 897092 | tf_op jit(solution)/shard_map/while/body/eval_jaxpr/bmnj,bnrj->brm/dot_general | solution.py:137
  232.3 5.9 %fusion.84 = f32[12,8,32,128]{3,2,1,0:T(8,128)} fusion(f32[12,8,32,128]{3,2,1,0:T(8,128)} %get-tuple-element.149, s32[]{:T(128)S(6)} %copy.97, f32[8,8,128]{2,1,0:T(8,128)S(1)} %bitcast.156, f32[8,128]{1,0:T(8,128)} %get-tuple-element.132, f32[8,8,128]{2,1,0:T(8,128)S(1)} %bitcast.157, f32[8,8,128]{2,1,0:T(8,128)S(1)} %bitcast.158, ...), kind=kOutput, calls=%fused_computation.21.clone.1 | convolution fusion | flops 87293952 | bytes 897092 | tf_op jit(solution)/shard_map/while/body/eval_jaxpr/bmnj,bnrj->brm/dot_general | solution.py:137
  243.2 5.9 %fusion.84 = f32[12,8,32,128]{3,2,1,0:T(8,128)} fusion(f32[12,8,32,128]{3,2,1,0:T(8,128)} %get-tuple-element.149, s32[]{:T(128)S(6)} %copy.97, f32[8,8,128]{2,1,0:T(8,128)S(1)} %bitcast.156, f32[8,128]{1,0:T(8,128)} %get-tuple-element.132, f32[8,8,128]{2,1,0:T(8,128)S(1)} %bitcast.157, f32[8,8,128]{2,1,0:T(8,128)S(1)} %bitcast.158, ...), kind=kOutput, calls=%fused_computation.21.clone.1 | convolution fusion | flops 87293952 | bytes 897092 | tf_op jit(solution)/shard_map/while/body/eval_jaxpr/bmnj,bnrj->brm/dot_general | solution.py:137
  262.4 2.8 fusion.37
  266.5 4.0 %gather_fusion.2 = bf16[576,2048]{1,0:T(8,128)(2,1)} fusion(bf16[288,2048]{1,0:T(8,128)(2,1)S(1)} %pad_maximum_fusion, s32[1024]{0:T(1024)S(1)} %pad_clamp_fusion.3), kind=kCustom, calls=%fused_computation.2 | custom fusion | bytes 4720896 | tf_op jit(solution)/shard_map/jit(_take)/gather | solution.py:116
  270.4 11.7 %gather.23 = bf16[96,6,64,32]{3,2,1,0:T(8,128)(2,1)} reshape(bf16[576,2048]{1,0:T(8,128)(2,1)} %gather_fusion.2) | data formatting | bytes 4718592 | tf_op jit(solution)/shard_map/jit(_take)/gather | solution.py:116
  282.1 10.3 %bitcast_add_fusion.1 = f32[96,32,128]{2,1,0:T(8,128)} fusion(f32[12,8,32,128]{3,2,1,0:T(8,128)} %get-tuple-element.37, bf16[96,64,128]{2,1,0:T(8,128)(2,1)S(1)} %copy-done, f32[32,96,64]{2,0,1:T(8,128)S(1)} %copy-done.2, bf16[96,6,64,64]{3,2,1,0:T(8,128)(2,1)} %copy.71, bf16[96,6,64,32]{3,2,1,0:T(8,128)(2,1)} %gather.23, pred[96,6]{1,0:T(8,128)(4,1)S(1)} %copy-done.7, ...), kind=kOutput, calls=%fused_computation.44 | convolution fusion | flops 204472320 | bytes 12584640 | tf_op jit(solution)/shard_map/lkr,lkm->lrm/dot_general | solution.py:127
  (204 shorter events, 90.5 us)
Async XLA Ops:
  0.0 282.1 %copy-start = (bf16[96,64,128]{2,1,0:T(8,128)(2,1)S(1)}, bf16[96,64,128]{2,1,0:T(8,128)(2,1)}, u32[]{:S(2)}) copy-start(bf16[96,64,128]{2,1,0:T(8,128)(2,1)} %param.25) | copy-start | bytes 4718596
  4.9 260.2 %collective-permute-start.1 = (bf16[96,2048]{1,0:T(8,128)(2,1)}, bf16[96,2048]{1,0:T(8,128)(2,1)}, u32[]{:S(2)}, u32[]{:S(2)}) collective-permute-start(bf16[96,2048]{1,0:T(8,128)(2,1)} %copy.66), channel_id=1, source_target_pairs={{1,0},{2,1},{3,2},{4,3},{5,4},{6,5},{7,6},{8,7},{9,8},{10,9},{11,1... | collective-permute-start | bytes 1179656 | tf_op jit(solution)/shard_map/ppermute | solution.py:29
  14.2 250.9 %collective-permute-start = (bf16[96,2048]{1,0:T(8,128)(2,1)}, bf16[96,2048]{1,0:T(8,128)(2,1)}, u32[]{:S(2)}, u32[]{:S(2)}) collective-permute-start(bf16[96,2048]{1,0:T(8,128)(2,1)} %copy.66), channel_id=1, source_target_pairs={{0,1},{1,2},{2,3},{3,4},{4,5},{5,6},{6,7},{7,8},{8,9},{9,10},{10,1... | collective-permute-start | bytes 1179656 | tf_op jit(solution)/shard_map/ppermute | solution.py:27
  16.9 97.5 %collective-permute-start.4 = (bf16[4,32,128]{2,1,0:T(8,128)(2,1)S(1)}, bf16[4,32,128]{2,1,0:T(8,128)(2,1)S(1)}, u32[]{:S(2)}, u32[]{:S(2)}) collective-permute-start(bf16[4,32,128]{2,1,0:T(8,128)(2,1)S(1)} %get-tuple-element.80), channel_id=1, source_target_pairs={{0,1},{1,2},{2,3},{3,4},{4,5},{5,6},{6,7},{7,8},{8,9},{9,10},{10,1... | collective-permute-start | bytes 98312 | tf_op jit(solution)/shard_map/ppermute | solution.py:27
  20.0 87.0 %collective-permute-start.6 = (f32[4,7,128]{2,1,0:T(8,128)S(1)}, f32[4,7,128]{2,1,0:T(8,128)S(1)}, u32[]{:S(2)}, u32[]{:S(2)}) collective-permute-start(f32[4,7,128]{2,1,0:T(8,128)S(1)} %get-tuple-element.82), channel_id=1, source_target_pairs={{0,1},{1,2},{2,3},{3,4},{4,5},{5,6},{6,7},{7,8},{8,9},{9,10},{10,1... | collective-permute-start | bytes 43016 | tf_op jit(solution)/shard_map/ppermute | solution.py:27
  22.0 13.9 %copy-start.6 = (bf16[1,64,64]{2,1,0:T(8,128)(2,1)S(1)}, bf16[1,64,64]{2,1,0:T(8,128)(2,1)}, u32[]{:S(2)}) copy-start(bf16[1,64,64]{2,1,0:T(8,128)(2,1)} %param.31) | copy-start | bytes 24580
  22.0 89.0 %collective-permute-start.7 = (f32[4,7,128]{2,1,0:T(8,128)S(1)}, f32[4,7,128]{2,1,0:T(8,128)S(1)}, u32[]{:S(2)}, u32[]{:S(2)}) collective-permute-start(f32[4,7,128]{2,1,0:T(8,128)S(1)} %get-tuple-element.83), channel_id=1, source_target_pairs={{1,0},{2,1},{3,2},{4,3},{5,4},{6,5},{7,6},{8,7},{9,8},{10,9},{11,1... | collective-permute-start | bytes 43016 | tf_op jit(solution)/shard_map/ppermute | solution.py:29
  33.8 34.7 %copy-start.11 = (s32[1,6]{1,0:T(1,128)S(1)}, s32[1,6]{1,0:T(1,128)}, u32[]{:S(2)}) copy-start(s32[1,6]{1,0:T(1,128)} %param.34) | copy-start | bytes 76
  33.9 35.4 %copy-start.12 = (s32[1,6]{1,0:T(1,128)S(1)}, s32[1,6]{1,0:T(1,128)}, u32[]{:S(2)}) copy-start(s32[1,6]{1,0:T(1,128)} %param.38) | copy-start | bytes 76
  33.9 37.1 %copy-start.8 = (s32[96,6]{0,1:T(8,128)S(1)}, s32[96,6]{0,1:T(8,128)}, u32[]{:S(2)}) copy-start(s32[96,6]{0,1:T(8,128)} %param.29) | copy-start | bytes 6916
  33.9 37.9 %copy-start.10 = (s32[96]{0:T(128)S(1)}, s32[96]{0:T(128)}, u32[]{:S(2)}) copy-start(s32[96]{0:T(128)} %param.30) | copy-start | bytes 1156
  33.9 38.5 %copy-start.9 = (s32[96,8]{0,1:T(8,128)S(1)}, s32[96,8]{0,1:T(8,128)}, u32[]{:S(2)}) copy-start(s32[96,8]{0,1:T(8,128)} %param.23) | copy-start | bytes 9220
  62.9 190.4 %all-to-all-start = ((bf16[32,2,1024]{2,1,0:T(2,128)(2,1)}), bf16[32,2,1024]{2,1,0:T(2,128)(2,1)}, u32[]{:S(2)}, u32[]{:S(2)}) async-start(bf16[32,2,1024]{2,1,0:T(2,128)(2,1)} %reshape.262), calls=%async_computation | async-start | bytes 262144 | tf_op jit(solution)/shard_map/all_to_all | solution.py:16
  107.0 10.1 %collective-permute-start.5 = (bf16[4,32,128]{2,1,0:T(8,128)(2,1)S(1)}, bf16[4,32,128]{2,1,0:T(8,128)(2,1)S(1)}, u32[]{:S(2)}, u32[]{:S(2)}) collective-permute-start(bf16[4,32,128]{2,1,0:T(8,128)(2,1)S(1)} %get-tuple-element.81), channel_id=1, source_target_pairs={{1,0},{2,1},{3,2},{4,3},{5,4},{6,5},{7,6},{8,7},{9,8},{10,9},{11,1... | collective-permute-start | bytes 98312 | tf_op jit(solution)/shard_map/ppermute | solution.py:29
  111.0 138.1 %collective-permute-start.3 = (bf16[8,2048]{1,0:T(8,128)(2,1)}, bf16[8,2048]{1,0:T(8,128)(2,1)}, u32[]{:S(2)}, u32[]{:S(2)}) collective-permute-start(bf16[8,2048]{1,0:T(8,128)(2,1)} %bitcast.123), channel_id=1, source_target_pairs={{8,0},{16,8},{24,16},{32,24},{40,32},{48,40},{56,48},{64,56},{72,6... | collective-permute-start | bytes 98312 | tf_op jit(solution)/shard_map/ppermute | solution.py:29
  114.4 134.6 %collective-permute-start.2 = (bf16[8,2048]{1,0:T(8,128)(2,1)}, bf16[8,2048]{1,0:T(8,128)(2,1)}, u32[]{:S(2)}, u32[]{:S(2)}) collective-permute-start(bf16[8,2048]{1,0:T(8,128)(2,1)} %bitcast.123), channel_id=1, source_target_pairs={{0,8},{8,16},{16,24},{24,32},{32,40},{40,48},{48,56},{56,64},{64,7... | collective-permute-start | bytes 98312 | tf_op jit(solution)/shard_map/ppermute | solution.py:27
  249.1 10.9 %copy-start.13 = (pred[6]{0:T(512)(128)(4,1)S(1)}, pred[6]{0:T(512)(128)(4,1)}, u32[]{:S(2)}) copy-start(pred[6]{0:T(512)(128)(4,1)} %compare_and_fusion.2) | copy-start | bytes 22
  249.1 13.3 %copy-start.1 = (bf16[96,64,64]{2,1,0:T(8,128)(2,1)S(1)}, bf16[96,64,64]{2,1,0:T(8,128)(2,1)}, u32[]{:S(2)}) copy-start(bf16[96,64,64]{2,1,0:T(8,128)(2,1)} %copy.78) | copy-start | bytes 2359300
  255.4 7.0 %copy-start.3 = (f32[32,64]{1,0:T(8,128)S(1)}, f32[32,64]{1,0:T(8,128)}, u32[]{:S(2)}) copy-start(f32[32,64]{1,0:T(8,128)} %convolution_bitcast_fusion.3) | copy-start | bytes 24580
  255.4 7.0 %copy-start.5 = (bf16[1,64,64]{2,1,0:T(8,128)(2,1)S(1)}, bf16[1,64,64]{2,1,0:T(8,128)(2,1)}, u32[]{:S(2)}) copy-start(bf16[1,64,64]{2,1,0:T(8,128)(2,1)} %param.32) | copy-start | bytes 24580
  270.4 11.7 %copy-start.2 = (f32[32,96,64]{2,0,1:T(8,128)S(1)}, f32[32,96,64]{2,0,1:T(8,128)}, u32[]{:S(2)}) copy-start(f32[32,96,64]{2,0,1:T(8,128)} %fusion.37) | copy-start | bytes 2359300
  270.4 11.7 %copy-start.4 = (bf16[96,6]{1,0:T(8,128)(2,1)S(1)}, bf16[96,6]{1,0:T(8,128)(2,1)}, u32[]{:S(2)}) copy-start(bf16[96,6]{1,0:T(8,128)(2,1)} %fusion.49) | copy-start | bytes 3460
  270.4 11.7 %copy-start.7 = (pred[96,6]{1,0:T(8,128)(4,1)S(1)}, pred[96,6]{1,0:T(8,128)(4,1)}, u32[]{:S(2)}) copy-start(pred[96,6]{1,0:T(8,128)(4,1)} %copy.64) | copy-start | bytes 1732
